TPU v7x, 32 devices: a whole 2x2x4 slice. The times are simulated.
32 devices in a mesh: groups: 2 (over y), segment: 4 (over z), inner: 4 (over x, core).
Axes of the slice: x: 2, y: 2, z: 4, core: 2. Of those that a mesh axis runs over, the one named last changes fastest.
Arguments:
- tokens: int32 [3, 64], P(None, 'groups'), parts along dimension 1, may hold values from 0 to 511
- embedding: bfloat16 [512, 4096], P(None, 'inner'), may hold values from -6 to 6
- in_proj: bfloat16 [4, 3, 4096, 4096], P('segment', None, None, 'inner'), may hold values from -0.09375 to 0.09375
- out_proj: bfloat16 [4, 4096, 4096], P('segment', 'inner'), may hold values from -0.09375 to 0.09375
- norm_gain: float32 [4, 4096], P('segment'), may hold values from 0.1 to 1.9
- fir_taps: float32 [4, 7, 4096], P('segment', None, 'inner'), may hold values from -2 to 2
- modal_rate: float32 [4, 8, 4096], P('segment', None, 'inner'), may hold values from 0.05 to 3
- modal_residue: float32 [4, 8, 4096], P('segment', None, 'inner'), may hold values from -2 to 2
- fir_state: float32 [4, 64, 6, 4096], P('segment', 'groups', None, 'inner'), parts along dimension 1, may hold values from -6 to 6
- modal_state: float32 [4, 64, 8, 4096], P('segment', 'groups', None, 'inner'), parts along dimension 1, may hold values from -6 to 6
- final_gain: float32 [4096], replicated, may hold values from 0.1 to 1.9
- unembed: bfloat16 [4096, 512], P(None, 'inner'), may hold values from -0.25 to 0.25
Outputs:
- logits: float32 [2, 64, 512], P(None, ('groups', 'segment'), 'inner'), parts along dimension 1
- logprob: float32 [2, 64], P(None, ('groups', 'segment')), parts along dimension 1
- fir_state_out: float32 [4, 64, 6, 4096], P('segment', 'groups', None, 'inner'), parts along dimension 1
- modal_state_out: float32 [4, 64, 8, 4096], P('segment', 'groups', None, 'inner'), parts along dimension 1
There are 2 independent parts, one for each index of `groups`. A program takes and returns all parts, laid end to end along the dimension named above; an argument that names none is the same for every part. Nothing has to cross between parts.
All inputs are finite; a program needn't handle non-finite values.
Results may differ from a plain program's by a relative error of at most 0.025.
Values may be sent and summed in bfloat16 or wider, within the bound.
No kernel may reach another device: no remote copies, remote signals or barrier semaphores. Data moves between devices by JAX's collectives and lax.ppermute only.
A program may use at most 128 MiB of HBM per device.

v0:
```python
import jax
import jax.numpy as jnp
from jax import lax
from jax.sharding import PartitionSpec as P

MICRO = 2


def from_behind(block, axis, distance):
    devices = range(lax.axis_size(axis))
    route = [(i - distance, i) for i in devices if i - distance in devices]
    return lax.ppermute(block, axis, route)


def normed(values, scale_gain):
    mean_square = jnp.mean(values * values, axis=-1, keepdims=True)
    return values * lax.rsqrt(mean_square + 1e-05) * scale_gain


def short_filter(operands):
    product, fir_rows, modal_rows, taps_local, rate_local, residue_local = operands
    window = jnp.concatenate([fir_rows, product[:, None, :]], axis=1)
    filtered = jnp.sum(window * taps_local[::-1][None], axis=1)
    return (filtered, window[:, 1:], modal_rows)


def modal_filter(operands):
    product, fir_rows, modal_rows, taps_local, rate_local, residue_local = operands
    decay_factor = jnp.exp(-rate_local)
    mode_values = decay_factor[None] * modal_rows + (1.0 - decay_factor[None]) * product[:, None, :]
    filtered = jnp.sum(residue_local[None] * mode_values, axis=1) + taps_local[0][None] * product
    return (filtered, fir_rows, mode_values)


def per_device(
    tokens,
    embedding,
    in_proj,
    out_proj,
    norm_gain,
    fir_taps,
    modal_rate,
    modal_residue,
    fir_state,
    modal_state,
    final_gain,
    unembed,
):
    segment_count = lax.axis_size("segment")
    segment_index = lax.axis_index("segment")
    inner_index = lax.axis_index("inner")
    step_count = tokens.shape[0] - 1
    seq_count = tokens.shape[1]
    block_count = MICRO
    row_count = seq_count // block_count
    item_count = step_count * block_count
    tick_count = item_count + segment_count - 1
    local_width = embedding.shape[1]
    w_in = in_proj[0]
    w_out = out_proj[0]
    gain_local = norm_gain[0]
    taps_local = fir_taps[0]
    rate_local = modal_rate[0]
    residue_local = modal_residue[0]
    is_short = segment_index % 2 == 0
    is_last = segment_index == segment_count - 1

    def advance(carry, tick_index):
        previous, fir_all, modal_all, recorded = carry
        item_index = tick_index - segment_index
        is_valid = (item_index >= 0) & (item_index < item_count)
        clipped = jnp.clip(item_index, 0, item_count - 1)
        step_index = clipped // block_count
        row_start = clipped % block_count * row_count
        incoming = from_behind(previous, "segment", 1)
        token_ids = lax.dynamic_slice(tokens, (step_index, row_start), (1, row_count))[0]
        looked_up = jnp.take(embedding, token_ids, axis=0)
        stream_in = jnp.where(segment_index == 0, looked_up, incoming)
        gathered = lax.all_gather(stream_in, "inner", axis=1, tiled=True)
        normalized = normed(gathered.astype(jnp.float32), gain_local).astype(jnp.bfloat16)
        projected = jnp.einsum("bd,jdc->jbc", normalized, w_in, preferred_element_type=jnp.float32)
        product = projected[1] * projected[2]
        fir_rows = lax.dynamic_slice_in_dim(fir_all, row_start, row_count, 0)
        modal_rows = lax.dynamic_slice_in_dim(modal_all, row_start, row_count, 0)
        filtered, fir_next, modal_next = lax.cond(
            is_short,
            short_filter,
            modal_filter,
            (product, fir_rows, modal_rows, taps_local, rate_local, residue_local),
        )
        fir_all = lax.dynamic_update_slice_in_dim(
            fir_all, jnp.where(is_valid, fir_next, fir_rows), row_start, 0
        )
        modal_all = lax.dynamic_update_slice_in_dim(
            modal_all, jnp.where(is_valid, modal_next, modal_rows), row_start, 0
        )
        gated_rows = (projected[0] * filtered).astype(jnp.bfloat16)
        partial_sum = jnp.dot(gated_rows, w_out, preferred_element_type=jnp.float32)
        mixed_sum = lax.psum_scatter(partial_sum, "inner", scatter_dimension=1, tiled=True)
        stream_out = (stream_in.astype(jnp.float32) + mixed_sum).astype(jnp.bfloat16)
        current = lax.dynamic_slice(
            recorded, (step_index, row_start, jnp.int32(0)), (1, row_count, local_width)
        )
        recorded = lax.dynamic_update_slice(
            recorded,
            jnp.where(is_valid & is_last, stream_out[None], current),
            (step_index, row_start, jnp.int32(0)),
        )
        return ((stream_out, fir_all, modal_all, recorded), None)

    initial = (
        jnp.zeros((row_count, local_width), jnp.bfloat16),
        fir_state[0],
        modal_state[0],
        jnp.zeros((step_count, seq_count, local_width), jnp.bfloat16),
    )
    final_carry, unused = lax.scan(advance, initial, jnp.arange(tick_count, dtype=jnp.int32))
    last_out, fir_final, modal_final, recorded = final_carry
    final_stream = lax.all_gather(recorded, "inner", axis=2, tiled=True)
    head_in = normed(final_stream.astype(jnp.float32), final_gain).astype(jnp.bfloat16)
    logits = jnp.einsum("tsd,dv->tsv", head_in, unembed, preferred_element_type=jnp.float32)
    vocab_local = unembed.shape[1]
    columns = inner_index * vocab_local + jnp.arange(vocab_local, dtype=jnp.int32)
    targets = tokens[1:]
    exp_local = jnp.sum(jnp.exp(logits), axis=-1)
    target_part = jnp.sum(
        jnp.where(columns[None, None, :] == targets[:, :, None], logits, 0.0), axis=-1
    )
    exp_total, target_logit = lax.psum((exp_local, target_part), "inner")
    logprob = target_logit - jnp.log(exp_total)
    logits_kept = jnp.where(is_last, logits, 0.0)
    logprob_kept = jnp.where(is_last, logprob, 0.0)
    logits_out, logprob_out = (
        lax.psum_scatter(logits_kept, "segment", scatter_dimension=1, tiled=True),
        lax.psum_scatter(logprob_kept, "segment", scatter_dimension=1, tiled=True),
    )
    return (logits_out, logprob_out, fir_final[None], modal_final[None])


def solution(mesh):
    return jax.shard_map(
        per_device,
        mesh=mesh,
        in_specs=(
            P(None, "groups"),
            P(None, "inner"),
            P("segment", None, None, "inner"),
            P("segment", "inner", None),
            P("segment", None),
            P("segment", None, "inner"),
            P("segment", None, "inner"),
            P("segment", None, "inner"),
            P("segment", "groups", None, "inner"),
            P("segment", "groups", None, "inner"),
            P(),
            P(None, "inner"),
        ),
        out_specs=(
            P(None, ("groups", "segment"), "inner"),
            P(None, ("groups", "segment")),
            P("segment", "groups", None, "inner"),
            P("segment", "groups", None, "inner"),
        ),
        check_vma=False,
    )
```

profile of v0, /device:TPU:0, one launch (start us, length us, event | category | flops | bytes accessed | tf_op | source)
XLA Modules:
  0.0 421.6 jit_solution(7223854443020577943)
XLA Ops:
  8.0 2.4 copy.56
  10.4 2.6 copy.26
  14.5 369.0 %while.19 = (s32[]{:T(128)}, bf16[16,1024]{1,0:T(8,128)(2,1)S(1)}, f32[32,6,1024]{2,1,0:T(8,128)}, f32[32,8,1024]{2,1,0:T(8,128)}, bf16[2,32,1024]{2,1,0:T(8,128...) while((s32[]{:T(128)}, bf16[16,1024]{1,0:T(8,128)(2,1)S(1)}, ...), condition=%wide.region_7.8_spmd.clone, body=%wide.region_0.7_spmd.clone.sunk | while | flops 538412224 | bytes 43820432 | solution.py:117
  14.6 5.0 %collective-permute-start = (bf16[16,1024]{1,0:T(8,128)(2,1)S(1)}, bf16[16,1024]{1,0:T(8,128)(2,1)S(1)}, u32[]{:S(2)}, u32[]{:S(2)}) collective-permute-start(bf16[16,1024]{1,0:T(8,128)(2,1)S(1)} %broadcast_select_fusion.3), channel_id=1, source_target_pairs={{0,4},{4,8},{8,12},{1,5},{5,9},{9,13},{2,6},{6,10},{10,14},{3,7},{... | collective-permute-start | bytes 98312 | tf_op jit(solution)/shard_map/while/body/eval_jaxpr/ppermute | solution.py:12
  24.5 2.0 gather_fusion
  26.6 5.4 %all_gather.12 = bf16[16,4096]{1,0:T(8,128)(2,1)S(1)} all-gather(bf16[16,1024]{1,0:T(8,128)(2,1)S(1)} %select_select_fusion.2), channel_id=1, replica_groups=mesh['groups'=2,'segment'=4,'inner'=4] {'inner'}, dimensions={1}, use_global_device_ids=true | all-gather | bytes 163840 | tf_op jit(solution)/shard_map/while/body/eval_jaxpr/all_gather | solution.py:79
  32.2 10.0 %convolution_bitcast_fusion.2 = f32[3,16,1024]{2,1,0:T(8,128)S(1)} fusion(bf16[3,4096,1024]{2,1,0:T(8,128)(2,1)} %get-tuple-element.555, bf16[16,4096]{1,0:T(8,128)(2,1)S(1)} %all_gather.12, f32[4096]{0:T(1024)} %bitcast.78, f32[16]{0:T(128)S(1)} %add_rsqrt_fusion.3), kind=kOutput, calls=%fused_computation.11.clone.1 | convolution fusion | flops 402915328 | bytes 25509952 | tf_op jit(solution)/shard_map/while/body/eval_jaxpr/bd,jdc->jbc/dot_general | solution.py:81
  42.9 5.3 %fusion.43 = f32[16,4096]{1,0:T(8,128)} fusion(bf16[1024,4096]{1,0:T(8,128)(2,1)} %get-tuple-element.560, f32[16,1024]{1,0:T(8,128)S(1)} %get-tuple-element.481, f32[3,16,1024]{2,1,0:T(8,128)S(1)} %convolution_bitcast_fusion.2), kind=kOutput, calls=%fused_computation.28.clone.1 | convolution fusion | flops 134250496 | bytes 8781824 | tf_op jit(solution)/shard_map/while/body/eval_jaxpr/dot_general | solution.py:98
  48.2 1.9 select_dynamic-update-slice_fusion.4
  50.1 1.9 select_dynamic-update-slice_fusion.5
  52.0 16.6 %reduce-scatter.6.cloned.1.call-done = f32[16,1024]{1,0:T(8,128)} async-done(((f32[16,4096]{1,0:T(8,128)}), f32[16,1024]{1,0:T(8,128)}) %reduce-scatter.6.cloned.1.call-update) | async-done | bytes 65552 | tf_op jit(solution)/shard_map/while/body/eval_jaxpr/reduce_scatter | solution.py:99
  69.6 3.4 collective-permute-start
  78.0 2.0 gather_fusion
  80.1 5.4 %all_gather.12 = bf16[16,4096]{1,0:T(8,128)(2,1)S(1)} all-gather(bf16[16,1024]{1,0:T(8,128)(2,1)S(1)} %select_select_fusion.2), channel_id=1, replica_groups=mesh['groups'=2,'segment'=4,'inner'=4] {'inner'}, dimensions={1}, use_global_device_ids=true | all-gather | bytes 163840 | tf_op jit(solution)/shard_map/while/body/eval_jaxpr/all_gather | solution.py:79
  85.6 10.0 %convolution_bitcast_fusion.2 = f32[3,16,1024]{2,1,0:T(8,128)S(1)} fusion(bf16[3,4096,1024]{2,1,0:T(8,128)(2,1)} %get-tuple-element.555, bf16[16,4096]{1,0:T(8,128)(2,1)S(1)} %all_gather.12, f32[4096]{0:T(1024)} %bitcast.78, f32[16]{0:T(128)S(1)} %add_rsqrt_fusion.3), kind=kOutput, calls=%fused_computation.11.clone.1 | convolution fusion | flops 402915328 | bytes 25509952 | tf_op jit(solution)/shard_map/while/body/eval_jaxpr/bd,jdc->jbc/dot_general | solution.py:81
  96.4 5.3 %fusion.43 = f32[16,4096]{1,0:T(8,128)} fusion(bf16[1024,4096]{1,0:T(8,128)(2,1)} %get-tuple-element.560, f32[16,1024]{1,0:T(8,128)S(1)} %get-tuple-element.481, f32[3,16,1024]{2,1,0:T(8,128)S(1)} %convolution_bitcast_fusion.2), kind=kOutput, calls=%fused_computation.28.clone.1 | convolution fusion | flops 134250496 | bytes 8781824 | tf_op jit(solution)/shard_map/while/body/eval_jaxpr/dot_general | solution.py:98
  101.7 1.9 select_dynamic-update-slice_fusion.4
  103.6 1.9 select_dynamic-update-slice_fusion.5
  105.5 15.5 %reduce-scatter.6.cloned.1.call-done = f32[16,1024]{1,0:T(8,128)} async-done(((f32[16,4096]{1,0:T(8,128)}), f32[16,1024]{1,0:T(8,128)}) %reduce-scatter.6.cloned.1.call-update) | async-done | bytes 65552 | tf_op jit(solution)/shard_map/while/body/eval_jaxpr/reduce_scatter | solution.py:99
  121.9 3.4 collective-permute-start
  128.5 1.1 constant_dynamic-slice_fusion.6
  130.3 2.0 gather_fusion
  132.4 5.4 %all_gather.12 = bf16[16,4096]{1,0:T(8,128)(2,1)S(1)} all-gather(bf16[16,1024]{1,0:T(8,128)(2,1)S(1)} %select_select_fusion.2), channel_id=1, replica_groups=mesh['groups'=2,'segment'=4,'inner'=4] {'inner'}, dimensions={1}, use_global_device_ids=true | all-gather | bytes 163840 | tf_op jit(solution)/shard_map/while/body/eval_jaxpr/all_gather | solution.py:79
  138.0 10.0 %convolution_bitcast_fusion.2 = f32[3,16,1024]{2,1,0:T(8,128)S(1)} fusion(bf16[3,4096,1024]{2,1,0:T(8,128)(2,1)} %get-tuple-element.555, bf16[16,4096]{1,0:T(8,128)(2,1)S(1)} %all_gather.12, f32[4096]{0:T(1024)} %bitcast.78, f32[16]{0:T(128)S(1)} %add_rsqrt_fusion.3), kind=kOutput, calls=%fused_computation.11.clone.1 | convolution fusion | flops 402915328 | bytes 25509952 | tf_op jit(solution)/shard_map/while/body/eval_jaxpr/bd,jdc->jbc/dot_general | solution.py:81
  148.7 5.3 %fusion.43 = f32[16,4096]{1,0:T(8,128)} fusion(bf16[1024,4096]{1,0:T(8,128)(2,1)} %get-tuple-element.560, f32[16,1024]{1,0:T(8,128)S(1)} %get-tuple-element.481, f32[3,16,1024]{2,1,0:T(8,128)S(1)} %convolution_bitcast_fusion.2), kind=kOutput, calls=%fused_computation.28.clone.1 | convolution fusion | flops 134250496 | bytes 8781824 | tf_op jit(solution)/shard_map/while/body/eval_jaxpr/dot_general | solution.py:98
  154.0 1.9 select_dynamic-update-slice_fusion.4
  155.9 1.9 select_dynamic-update-slice_fusion.5
  157.8 15.5 %reduce-scatter.6.cloned.1.call-done = f32[16,1024]{1,0:T(8,128)} async-done(((f32[16,4096]{1,0:T(8,128)}), f32[16,1024]{1,0:T(8,128)}) %reduce-scatter.6.cloned.1.call-update) | async-done | bytes 65552 | tf_op jit(solution)/shard_map/while/body/eval_jaxpr/reduce_scatter | solution.py:99
  174.3 3.4 collective-permute-start
  182.6 2.0 gather_fusion
  184.7 5.4 %all_gather.12 = bf16[16,4096]{1,0:T(8,128)(2,1)S(1)} all-gather(bf16[16,1024]{1,0:T(8,128)(2,1)S(1)} %select_select_fusion.2), channel_id=1, replica_groups=mesh['groups'=2,'segment'=4,'inner'=4] {'inner'}, dimensions={1}, use_global_device_ids=true | all-gather | bytes 163840 | tf_op jit(solution)/shard_map/while/body/eval_jaxpr/all_gather | solution.py:79
  190.3 10.0 %convolution_bitcast_fusion.2 = f32[3,16,1024]{2,1,0:T(8,128)S(1)} fusion(bf16[3,4096,1024]{2,1,0:T(8,128)(2,1)} %get-tuple-element.555, bf16[16,4096]{1,0:T(8,128)(2,1)S(1)} %all_gather.12, f32[4096]{0:T(1024)} %bitcast.78, f32[16]{0:T(128)S(1)} %add_rsqrt_fusion.3), kind=kOutput, calls=%fused_computation.11.clone.1 | convolution fusion | flops 402915328 | bytes 25509952 | tf_op jit(solution)/shard_map/while/body/eval_jaxpr/bd,jdc->jbc/dot_general | solution.py:81
  201.0 5.3 %fusion.43 = f32[16,4096]{1,0:T(8,128)} fusion(bf16[1024,4096]{1,0:T(8,128)(2,1)} %get-tuple-element.560, f32[16,1024]{1,0:T(8,128)S(1)} %get-tuple-element.481, f32[3,16,1024]{2,1,0:T(8,128)S(1)} %convolution_bitcast_fusion.2), kind=kOutput, calls=%fused_computation.28.clone.1 | convolution fusion | flops 134250496 | bytes 8781824 | tf_op jit(solution)/shard_map/while/body/eval_jaxpr/dot_general | solution.py:98
  206.4 1.9 select_dynamic-update-slice_fusion.4
  208.3 1.9 select_dynamic-update-slice_fusion.5
  210.2 15.5 %reduce-scatter.6.cloned.1.call-done = f32[16,1024]{1,0:T(8,128)} async-done(((f32[16,4096]{1,0:T(8,128)}), f32[16,1024]{1,0:T(8,128)}) %reduce-scatter.6.cloned.1.call-update) | async-done | bytes 65552 | tf_op jit(solution)/shard_map/while/body/eval_jaxpr/reduce_scatter | solution.py:99
  226.6 3.4 collective-permute-start
  235.0 2.0 gather_fusion
  237.0 5.4 %all_gather.12 = bf16[16,4096]{1,0:T(8,128)(2,1)S(1)} all-gather(bf16[16,1024]{1,0:T(8,128)(2,1)S(1)} %select_select_fusion.2), channel_id=1, replica_groups=mesh['groups'=2,'segment'=4,'inner'=4] {'inner'}, dimensions={1}, use_global_device_ids=true | all-gather | bytes 163840 | tf_op jit(solution)/shard_map/while/body/eval_jaxpr/all_gather | solution.py:79
  242.6 10.0 %convolution_bitcast_fusion.2 = f32[3,16,1024]{2,1,0:T(8,128)S(1)} fusion(bf16[3,4096,1024]{2,1,0:T(8,128)(2,1)} %get-tuple-element.555, bf16[16,4096]{1,0:T(8,128)(2,1)S(1)} %all_gather.12, f32[4096]{0:T(1024)} %bitcast.78, f32[16]{0:T(128)S(1)} %add_rsqrt_fusion.3), kind=kOutput, calls=%fused_computation.11.clone.1 | convolution fusion | flops 402915328 | bytes 25509952 | tf_op jit(solution)/shard_map/while/body/eval_jaxpr/bd,jdc->jbc/dot_general | solution.py:81
  253.3 5.3 %fusion.43 = f32[16,4096]{1,0:T(8,128)} fusion(bf16[1024,4096]{1,0:T(8,128)(2,1)} %get-tuple-element.560, f32[16,1024]{1,0:T(8,128)S(1)} %get-tuple-element.481, f32[3,16,1024]{2,1,0:T(8,128)S(1)} %convolution_bitcast_fusion.2), kind=kOutput, calls=%fused_computation.28.clone.1 | convolution fusion | flops 134250496 | bytes 8781824 | tf_op jit(solution)/shard_map/while/body/eval_jaxpr/dot_general | solution.py:98
  258.7 1.9 select_dynamic-update-slice_fusion.4
  260.6 1.9 select_dynamic-update-slice_fusion.5
  262.5 15.5 %reduce-scatter.6.cloned.1.call-done = f32[16,1024]{1,0:T(8,128)} async-done(((f32[16,4096]{1,0:T(8,128)}), f32[16,1024]{1,0:T(8,128)}) %reduce-scatter.6.cloned.1.call-update) | async-done | bytes 65552 | tf_op jit(solution)/shard_map/while/body/eval_jaxpr/reduce_scatter | solution.py:99
  278.9 3.4 collective-permute-start
  287.3 2.0 gather_fusion
  289.4 5.4 %all_gather.12 = bf16[16,4096]{1,0:T(8,128)(2,1)S(1)} all-gather(bf16[16,1024]{1,0:T(8,128)(2,1)S(1)} %select_select_fusion.2), channel_id=1, replica_groups=mesh['groups'=2,'segment'=4,'inner'=4] {'inner'}, dimensions={1}, use_global_device_ids=true | all-gather | bytes 163840 | tf_op jit(solution)/shard_map/while/body/eval_jaxpr/all_gather | solution.py:79
  294.9 10.0 %convolution_bitcast_fusion.2 = f32[3,16,1024]{2,1,0:T(8,128)S(1)} fusion(bf16[3,4096,1024]{2,1,0:T(8,128)(2,1)} %get-tuple-element.555, bf16[16,4096]{1,0:T(8,128)(2,1)S(1)} %all_gather.12, f32[4096]{0:T(1024)} %bitcast.78, f32[16]{0:T(128)S(1)} %add_rsqrt_fusion.3), kind=kOutput, calls=%fused_computation.11.clone.1 | convolution fusion | flops 402915328 | bytes 25509952 | tf_op jit(solution)/shard_map/while/body/eval_jaxpr/bd,jdc->jbc/dot_general | solution.py:81
  305.7 5.3 %fusion.43 = f32[16,4096]{1,0:T(8,128)} fusion(bf16[1024,4096]{1,0:T(8,128)(2,1)} %get-tuple-element.560, f32[16,1024]{1,0:T(8,128)S(1)} %get-tuple-element.481, f32[3,16,1024]{2,1,0:T(8,128)S(1)} %convolution_bitcast_fusion.2), kind=kOutput, calls=%fused_computation.28.clone.1 | convolution fusion | flops 134250496 | bytes 8781824 | tf_op jit(solution)/shard_map/while/body/eval_jaxpr/dot_general | solution.py:98
  311.0 1.9 select_dynamic-update-slice_fusion.4
  312.9 1.9 select_dynamic-update-slice_fusion.5
  314.8 15.5 %reduce-scatter.6.cloned.1.call-done = f32[16,1024]{1,0:T(8,128)} async-done(((f32[16,4096]{1,0:T(8,128)}), f32[16,1024]{1,0:T(8,128)}) %reduce-scatter.6.cloned.1.call-update) | async-done | bytes 65552 | tf_op jit(solution)/shard_map/while/body/eval_jaxpr/reduce_scatter | solution.py:99
  331.2 3.4 collective-permute-start
  339.6 2.0 gather_fusion
  341.7 5.4 %all_gather.12 = bf16[16,4096]{1,0:T(8,128)(2,1)S(1)} all-gather(bf16[16,1024]{1,0:T(8,128)(2,1)S(1)} %select_select_fusion.2), channel_id=1, replica_groups=mesh['groups'=2,'segment'=4,'inner'=4] {'inner'}, dimensions={1}, use_global_device_ids=true | all-gather | bytes 163840 | tf_op jit(solution)/shard_map/while/body/eval_jaxpr/all_gather | solution.py:79
  347.2 10.0 %convolution_bitcast_fusion.2 = f32[3,16,1024]{2,1,0:T(8,128)S(1)} fusion(bf16[3,4096,1024]{2,1,0:T(8,128)(2,1)} %get-tuple-element.555, bf16[16,4096]{1,0:T(8,128)(2,1)S(1)} %all_gather.12, f32[4096]{0:T(1024)} %bitcast.78, f32[16]{0:T(128)S(1)} %add_rsqrt_fusion.3), kind=kOutput, calls=%fused_computation.11.clone.1 | convolution fusion | flops 402915328 | bytes 25509952 | tf_op jit(solution)/shard_map/while/body/eval_jaxpr/bd,jdc->jbc/dot_general | solution.py:81
  358.0 5.3 %fusion.43 = f32[16,4096]{1,0:T(8,128)} fusion(bf16[1024,4096]{1,0:T(8,128)(2,1)} %get-tuple-element.560, f32[16,1024]{1,0:T(8,128)S(1)} %get-tuple-element.481, f32[3,16,1024]{2,1,0:T(8,128)S(1)} %convolution_bitcast_fusion.2), kind=kOutput, calls=%fused_computation.28.clone.1 | convolution fusion | flops 134250496 | bytes 8781824 | tf_op jit(solution)/shard_map/while/body/eval_jaxpr/dot_general | solution.py:98
  363.3 1.9 select_dynamic-update-slice_fusion.4
  365.3 1.9 select_dynamic-update-slice_fusion.5
  367.1 15.5 %reduce-scatter.6.cloned.1.call-done = f32[16,1024]{1,0:T(8,128)} async-done(((f32[16,4096]{1,0:T(8,128)}), f32[16,1024]{1,0:T(8,128)}) %reduce-scatter.6.cloned.1.call-update) | async-done | bytes 65552 | tf_op jit(solution)/shard_map/while/body/eval_jaxpr/reduce_scatter | solution.py:99
  383.5 6.5 %all_gather.9 = bf16[2,32,4096]{2,1,0:T(8,128)(2,1)S(1)} all-gather(bf16[2,32,1024]{2,1,0:T(8,128)(2,1)S(1)} %get-tuple-element.257), channel_id=1, replica_groups=mesh['groups'=2,'segment'=4,'inner'=4] {'inner'}, dimensions={2}, use_global_device_ids=true | all-gather | bytes 655360 | tf_op jit(solution)/shard_map/all_gather | solution.py:119
  391.3 2.6 copy.27
  393.8 6.7 %all-reduce.1 = (f32[2,32]{1,0:T(2,128)S(1)}, f32[2,32]{1,0:T(2,128)S(1)}) all-reduce(f32[2,32]{1,0:T(2,128)S(1)} %get-tuple-element.321, f32[2,32]{1,0:T(2,128)S(1)} %get-tuple-element.320), channel_id=1, replica_groups=mesh['groups'=2,'segment'=4,'inner'=4] {'inner'}, use_global_device_ids=true, to_apply=%region_11.12 | all-reduce | flops 128 | bytes 1024 | tf_op jit(solution)/shard_map/psum | solution.py:129
  400.6 11.7 %all-reduce = f32[2,32]{1,0:T(2,128)S(1)} all-reduce(f32[2,32]{1,0:T(2,128)S(1)} %subtract_select_fusion), channel_id=4, replica_groups=mesh['groups'=2,'segment'=4,'inner'=4] {'segment'}, use_global_device_ids=true, to_apply=%region_14.15.clone | all-reduce | flops 64 | bytes 512
  (195 shorter events, 51.1 us)
Async XLA Ops:
  8.0 382.3 %copy-start = (bf16[4096,128]{1,0:T(8,128)(2,1)S(1)}, bf16[4096,128]{1,0:T(8,128)(2,1)}, u32[]{:S(2)}) copy-start(bf16[4096,128]{1,0:T(8,128)(2,1)} %param.27) | copy-start | bytes 3145732
  14.5 375.8 %copy-start.3 = (f32[4096]{0:T(1024)S(1)}, f32[4096]{0:T(1024)}, u32[]{:S(2)}) copy-start(f32[4096]{0:T(1024)} %param.26) | copy-start | bytes 49156
  14.5 397.8 %copy-start.4 = (u32[32]{0:T(128)S(1)}, u32[32]{0:T(128)}, u32[]{:S(2)}) copy-start(u32[32]{0:T(128)} %constant.157) | copy-start | bytes 388
  14.5 54.2 %reduce-scatter.6.cloned.1.call-start = ((), (), s32[]{:S(2)}) async-start(), calls=%async_computation.3 | async-start | bytes 327680 | tf_op jit(solution)/shard_map/while/body/eval_jaxpr/reduce_scatter | solution.py:99
  14.6 11.9 %collective-permute-start = (bf16[16,1024]{1,0:T(8,128)(2,1)S(1)}, bf16[16,1024]{1,0:T(8,128)(2,1)S(1)}, u32[]{:S(2)}, u32[]{:S(2)}) collective-permute-start(bf16[16,1024]{1,0:T(8,128)(2,1)S(1)} %broadcast_select_fusion.3), channel_id=1, source_target_pairs={{0,4},{4,8},{8,12},{1,5},{5,9},{9,13},{2,6},{6,10},{10,14},{3,7},{... | collective-permute-start | bytes 98312 | tf_op jit(solution)/shard_map/while/body/eval_jaxpr/ppermute | solution.py:12
  26.5 15.7 %copy-start.1 = (f32[1,8,1024]{2,1,0:T(8,128)S(1)}, f32[1,8,1024]{2,1,0:T(8,128)}, u32[]{:S(2)}) copy-start(f32[1,8,1024]{2,1,0:T(8,128)} %get-tuple-element.557) | copy-start | bytes 98308 | tf_op jit(solution)/shard_map/while
  26.5 15.6 %copy-start.2 = (f32[8,1024]{1,0:T(8,128)S(1)}, f32[8,1024]{1,0:T(8,128)}, u32[]{:S(2)}) copy-start(f32[8,1024]{1,0:T(8,128)} %get-tuple-element.558) | copy-start | bytes 98308 | tf_op jit(solution)/shard_map/while
  69.5 51.5 %reduce-scatter.6.cloned.1.call-start = ((), (), s32[]{:S(2)}) async-start(), calls=%async_computation.3 | async-start | bytes 327680 | tf_op jit(solution)/shard_map/while/body/eval_jaxpr/reduce_scatter | solution.py:99
  69.6 10.4 %collective-permute-start = (bf16[16,1024]{1,0:T(8,128)(2,1)S(1)}, bf16[16,1024]{1,0:T(8,128)(2,1)S(1)}, u32[]{:S(2)}, u32[]{:S(2)}) collective-permute-start(bf16[16,1024]{1,0:T(8,128)(2,1)S(1)} %broadcast_select_fusion.3), channel_id=1, source_target_pairs={{0,4},{4,8},{8,12},{1,5},{5,9},{9,13},{2,6},{6,10},{10,14},{3,7},{... | collective-permute-start | bytes 98312 | tf_op jit(solution)/shard_map/while/body/eval_jaxpr/ppermute | solution.py:12
  80.0 15.7 %copy-start.1 = (f32[1,8,1024]{2,1,0:T(8,128)S(1)}, f32[1,8,1024]{2,1,0:T(8,128)}, u32[]{:S(2)}) copy-start(f32[1,8,1024]{2,1,0:T(8,128)} %get-tuple-element.557) | copy-start | bytes 98308 | tf_op jit(solution)/shard_map/while
  80.0 15.6 %copy-start.2 = (f32[8,1024]{1,0:T(8,128)S(1)}, f32[8,1024]{1,0:T(8,128)}, u32[]{:S(2)}) copy-start(f32[8,1024]{1,0:T(8,128)} %get-tuple-element.558) | copy-start | bytes 98308 | tf_op jit(solution)/shard_map/while
  121.9 51.5 %reduce-scatter.6.cloned.1.call-start = ((), (), s32[]{:S(2)}) async-start(), calls=%async_computation.3 | async-start | bytes 327680 | tf_op jit(solution)/shard_map/while/body/eval_jaxpr/reduce_scatter | solution.py:99
  121.9 10.4 %collective-permute-start = (bf16[16,1024]{1,0:T(8,128)(2,1)S(1)}, bf16[16,1024]{1,0:T(8,128)(2,1)S(1)}, u32[]{:S(2)}, u32[]{:S(2)}) collective-permute-start(bf16[16,1024]{1,0:T(8,128)(2,1)S(1)} %broadcast_select_fusion.3), channel_id=1, source_target_pairs={{0,4},{4,8},{8,12},{1,5},{5,9},{9,13},{2,6},{6,10},{10,14},{3,7},{... | collective-permute-start | bytes 98312 | tf_op jit(solution)/shard_map/while/body/eval_jaxpr/ppermute | solution.py:12
  132.3 15.7 %copy-start.1 = (f32[1,8,1024]{2,1,0:T(8,128)S(1)}, f32[1,8,1024]{2,1,0:T(8,128)}, u32[]{:S(2)}) copy-start(f32[1,8,1024]{2,1,0:T(8,128)} %get-tuple-element.557) | copy-start | bytes 98308 | tf_op jit(solution)/shard_map/while
  132.3 15.6 %copy-start.2 = (f32[8,1024]{1,0:T(8,128)S(1)}, f32[8,1024]{1,0:T(8,128)}, u32[]{:S(2)}) copy-start(f32[8,1024]{1,0:T(8,128)} %get-tuple-element.558) | copy-start | bytes 98308 | tf_op jit(solution)/shard_map/while
  174.2 51.4 %reduce-scatter.6.cloned.1.call-start = ((), (), s32[]{:S(2)}) async-start(), calls=%async_computation.3 | async-start | bytes 327680 | tf_op jit(solution)/shard_map/while/body/eval_jaxpr/reduce_scatter | solution.py:99
  174.3 10.4 %collective-permute-start = (bf16[16,1024]{1,0:T(8,128)(2,1)S(1)}, bf16[16,1024]{1,0:T(8,128)(2,1)S(1)}, u32[]{:S(2)}, u32[]{:S(2)}) collective-permute-start(bf16[16,1024]{1,0:T(8,128)(2,1)S(1)} %broadcast_select_fusion.3), channel_id=1, source_target_pairs={{0,4},{4,8},{8,12},{1,5},{5,9},{9,13},{2,6},{6,10},{10,14},{3,7},{... | collective-permute-start | bytes 98312 | tf_op jit(solution)/shard_map/while/body/eval_jaxpr/ppermute | solution.py:12
  184.6 15.7 %copy-start.1 = (f32[1,8,1024]{2,1,0:T(8,128)S(1)}, f32[1,8,1024]{2,1,0:T(8,128)}, u32[]{:S(2)}) copy-start(f32[1,8,1024]{2,1,0:T(8,128)} %get-tuple-element.557) | copy-start | bytes 98308 | tf_op jit(solution)/shard_map/while
  184.6 15.6 %copy-start.2 = (f32[8,1024]{1,0:T(8,128)S(1)}, f32[8,1024]{1,0:T(8,128)}, u32[]{:S(2)}) copy-start(f32[8,1024]{1,0:T(8,128)} %get-tuple-element.558) | copy-start | bytes 98308 | tf_op jit(solution)/shard_map/while
  226.5 51.4 %reduce-scatter.6.cloned.1.call-start = ((), (), s32[]{:S(2)}) async-start(), calls=%async_computation.3 | async-start | bytes 327680 | tf_op jit(solution)/shard_map/while/body/eval_jaxpr/reduce_scatter | solution.py:99
  226.6 10.4 %collective-permute-start = (bf16[16,1024]{1,0:T(8,128)(2,1)S(1)}, bf16[16,1024]{1,0:T(8,128)(2,1)S(1)}, u32[]{:S(2)}, u32[]{:S(2)}) collective-permute-start(bf16[16,1024]{1,0:T(8,128)(2,1)S(1)} %broadcast_select_fusion.3), channel_id=1, source_target_pairs={{0,4},{4,8},{8,12},{1,5},{5,9},{9,13},{2,6},{6,10},{10,14},{3,7},{... | collective-permute-start | bytes 98312 | tf_op jit(solution)/shard_map/while/body/eval_jaxpr/ppermute | solution.py:12
  236.9 15.7 %copy-start.1 = (f32[1,8,1024]{2,1,0:T(8,128)S(1)}, f32[1,8,1024]{2,1,0:T(8,128)}, u32[]{:S(2)}) copy-start(f32[1,8,1024]{2,1,0:T(8,128)} %get-tuple-element.557) | copy-start | bytes 98308 | tf_op jit(solution)/shard_map/while
  236.9 15.6 %copy-start.2 = (f32[8,1024]{1,0:T(8,128)S(1)}, f32[8,1024]{1,0:T(8,128)}, u32[]{:S(2)}) copy-start(f32[8,1024]{1,0:T(8,128)} %get-tuple-element.558) | copy-start | bytes 98308 | tf_op jit(solution)/shard_map/while
  278.8 51.4 %reduce-scatter.6.cloned.1.call-start = ((), (), s32[]{:S(2)}) async-start(), calls=%async_computation.3 | async-start | bytes 327680 | tf_op jit(solution)/shard_map/while/body/eval_jaxpr/reduce_scatter | solution.py:99
  278.9 10.4 %collective-permute-start = (bf16[16,1024]{1,0:T(8,128)(2,1)S(1)}, bf16[16,1024]{1,0:T(8,128)(2,1)S(1)}, u32[]{:S(2)}, u32[]{:S(2)}) collective-permute-start(bf16[16,1024]{1,0:T(8,128)(2,1)S(1)} %broadcast_select_fusion.3), channel_id=1, source_target_pairs={{0,4},{4,8},{8,12},{1,5},{5,9},{9,13},{2,6},{6,10},{10,14},{3,7},{... | collective-permute-start | bytes 98312 | tf_op jit(solution)/shard_map/while/body/eval_jaxpr/ppermute | solution.py:12
  289.2 15.7 %copy-start.1 = (f32[1,8,1024]{2,1,0:T(8,128)S(1)}, f32[1,8,1024]{2,1,0:T(8,128)}, u32[]{:S(2)}) copy-start(f32[1,8,1024]{2,1,0:T(8,128)} %get-tuple-element.557) | copy-start | bytes 98308 | tf_op jit(solution)/shard_map/while
  289.3 15.6 %copy-start.2 = (f32[8,1024]{1,0:T(8,128)S(1)}, f32[8,1024]{1,0:T(8,128)}, u32[]{:S(2)}) copy-start(f32[8,1024]{1,0:T(8,128)} %get-tuple-element.558) | copy-start | bytes 98308 | tf_op jit(solution)/shard_map/while
  331.2 51.4 %reduce-scatter.6.cloned.1.call-start = ((), (), s32[]{:S(2)}) async-start(), calls=%async_computation.3 | async-start | bytes 327680 | tf_op jit(solution)/shard_map/while/body/eval_jaxpr/reduce_scatter | solution.py:99
  331.2 10.4 %collective-permute-start = (bf16[16,1024]{1,0:T(8,128)(2,1)S(1)}, bf16[16,1024]{1,0:T(8,128)(2,1)S(1)}, u32[]{:S(2)}, u32[]{:S(2)}) collective-permute-start(bf16[16,1024]{1,0:T(8,128)(2,1)S(1)} %broadcast_select_fusion.3), channel_id=1, source_target_pairs={{0,4},{4,8},{8,12},{1,5},{5,9},{9,13},{2,6},{6,10},{10,14},{3,7},{... | collective-permute-start | bytes 98312 | tf_op jit(solution)/shard_map/while/body/eval_jaxpr/ppermute | solution.py:12
  341.6 15.7 %copy-start.1 = (f32[1,8,1024]{2,1,0:T(8,128)S(1)}, f32[1,8,1024]{2,1,0:T(8,128)}, u32[]{:S(2)}) copy-start(f32[1,8,1024]{2,1,0:T(8,128)} %get-tuple-element.557) | copy-start | bytes 98308 | tf_op jit(solution)/shard_map/while
  341.6 15.6 %copy-start.2 = (f32[8,1024]{1,0:T(8,128)S(1)}, f32[8,1024]{1,0:T(8,128)}, u32[]{:S(2)}) copy-start(f32[8,1024]{1,0:T(8,128)} %get-tuple-element.558) | copy-start | bytes 98308 | tf_op jit(solution)/shard_map/while
  383.5 30.7 %reduce-scatter.4.cloned.1.call-start = ((), (), s32[]{:S(2)}) async-start(), calls=%async_computation.2 | async-start | bytes 40960 | tf_op jit(solution)/shard_map/reduce_scatter | solution.py:134
Sparse Core Ops, SparseCore 0:
  48.3 20.2 reduce-scatter.5
  101.8 19.1 reduce-scatter.5
  154.1 19.1 reduce-scatter.5
  206.5 19.1 reduce-scatter.5
  258.8 19.1 reduce-scatter.5
  311.1 19.1 reduce-scatter.5
  363.4 19.1 reduce-scatter.5
Sparse Core Ops, SparseCore 1:
  391.4 19.8 reduce-scatter.3
where the time goes:
time: 425 us; the launch traced here: 422 us
  waiting for transfers between devices  110 us (26%)
  matrix products  108 us (25%)
  blocking collectives  62.8 us (15%)
  other arithmetic  48.1 us (11%)
  local copies, waits for them, and re-layouts  45.5 us (11%)
  starting transfers between devices  25.7 us (6%)
  between operations  16.2 us (4%)
  loops' own time  6.16 us (1%)
    reduce_scatter x7, waiting for transfers between devices, advance(): lax.psum_scatter(partial_sum, 'inner', scatter_dimension=1, tiled=True)  109 us
    dot_general x7, matrix products, advance(): jnp.einsum('bd,jdc->jbc', normalized, w_in, preferred_element_type=jnp.fl...  69.7 us
    all_gather x7, blocking collectives, advance(): gathered = lax.all_gather(stream_in, 'inner', axis=1, tiled=True)  37.8 us
    dot_general x7, matrix products, advance(): partial_sum = jnp.dot(gated_rows, w_out, preferred_element_type=jnp.float32)  37.1 us
    ppermute x7, starting transfers between devices, from_behind(): return lax.ppermute(block, axis, route)  25.3 us
    gather x7, local copies, waits for them, and re-layouts, advance(): looked_up = jnp.take(embedding, token_ids, axis=0)  13.8 us
    dynamic_update_slice x7, other arithmetic, advance(): lax.dynamic_update_slice_in_dim(fir_all, jnp.where(is_valid, fir_next, fi...  13.4 us
    dynamic_update_slice x7, other arithmetic, advance(): lax.dynamic_update_slice_in_dim(modal_all, jnp.where(is_valid, modal_next...  13.2 us
  transfers between devices with their start and end apart: 15, of which 7 were waited for; matrix products, arithmetic and copies ran while one was open for 18% of the time, Pallas kernels for 0%

commit v1 on v0

--- a/solution.py
+++ b/solution.py
@@ -76,7 +76,14 @@
         token_ids = lax.dynamic_slice(tokens, (step_index, row_start), (1, row_count))[0]
         looked_up = jnp.take(embedding, token_ids, axis=0)
         stream_in = jnp.where(segment_index == 0, looked_up, incoming)
-        gathered = lax.all_gather(stream_in, "inner", axis=1, tiled=True)
+        ring = [stream_in]
+        for hop in range(3):
+            ring.append(lax.ppermute(ring[-1], "inner", [(dev, (dev + 1) % 4) for dev in range(4)]))
+        gathered = jnp.roll(
+            jnp.concatenate(ring[::-1], axis=1),
+            (lax.axis_index("inner") + 1) * ring[0].shape[1],
+            axis=1,
+        )
         normalized = normed(gathered.astype(jnp.float32), gain_local).astype(jnp.bfloat16)
         projected = jnp.einsum("bd,jdc->jbc", normalized, w_in, preferred_element_type=jnp.float32)
         product = projected[1] * projected[2]

time: 425 us -> 442 us (1.040)
  waiting for transfers between devices: 110 us -> 164 us
  blocking collectives: 62.8 us -> 25 us
    ppermute x0 -> x21, waiting for transfers between devices: none -> 54.8 us  [advance(): lax.ppermute(ring[-1], 'inner', [(dev, (dev + 1) % 4) for dev in range(4)])]
    all_gather x7 -> x0, blocking collectives: 37.8 us -> none  [advance(): gathered = lax.all_gather(stream_in, 'inner', axis=1, tiled=True)]
  transfers between devices with their start and end apart: 15 -> 36, of which waited for: 7 -> 28; matrix products, arithmetic and copies ran while one was open for 18% -> 17% of each run, Pallas kernels for 0% -> 0%
where the time goes in v1:
time: 442 us; the launch traced here: 439 us
  waiting for transfers between devices  164 us (37%)
  matrix products  108 us (24%)
  other arithmetic  48.1 us (11%)
  local copies, waits for them, and re-layouts  45.6 us (10%)
  starting transfers between devices  25.7 us (6%)
  blocking collectives  25 us (6%)
  between operations  16.2 us (4%)
  loops' own time  6.65 us (2%)
    reduce_scatter x7, waiting for transfers between devices, advance(): lax.psum_scatter(partial_sum, 'inner', scatter_dimension=1, tiled=True)  109 us
    dot_general x7, matrix products, advance(): jnp.einsum('bd,jdc->jbc', normalized, w_in, preferred_element_type=jnp.fl...  69.7 us
    ppermute x21, waiting for transfers between devices, advance(): lax.ppermute(ring[-1], 'inner', [(dev, (dev + 1) % 4) for dev in range(4)])  54.8 us
    dot_general x7, matrix products, advance(): partial_sum = jnp.dot(gated_rows, w_out, preferred_element_type=jnp.float32)  37.1 us
    ppermute x7, starting transfers between devices, from_behind(): return lax.ppermute(block, axis, route)  25.3 us
    gather x7, local copies, waits for them, and re-layouts, advance(): looked_up = jnp.take(embedding, token_ids, axis=0)  13.8 us
    dynamic_update_slice x7, other arithmetic, advance(): lax.dynamic_update_slice_in_dim(fir_all, jnp.where(is_valid, fir_next, fi...  13.4 us
    dynamic_update_slice x7, other arithmetic, advance(): lax.dynamic_update_slice_in_dim(modal_all, jnp.where(is_valid, modal_next...  13.2 us
  transfers between devices with their start and end apart: 36, of which 28 were waited for; matrix products, arithmetic and copies ran while one was open for 17% of the time, Pallas kernels for 0%

profile of v1, /device:TPU:0, one launch (start us, length us, event | category | flops | bytes accessed | tf_op | source)
XLA Modules:
  0.0 439.3 jit_solution(1035222231934657969)
XLA Ops:
  8.0 2.4 copy.63
  10.4 2.6 copy.26
  14.5 386.7 %while.20 = (s32[]{:T(128)}, bf16[16,1024]{1,0:T(8,128)(2,1)S(1)}, f32[32,6,1024]{2,1,0:T(8,128)}, f32[32,8,1024]{2,1,0:T(8,128)}, bf16[2,32,1024]{2,1,0:T(8,128...) while((s32[]{:T(128)}, bf16[16,1024]{1,0:T(8,128)(2,1)S(1)}, ...), condition=%wide.region_7.8_spmd.clone, body=%wide.region_0.7_spmd.clone.sunk | while | flops 538412288 | bytes 44574912 | solution.py:124
  14.6 5.0 %collective-permute-start = (bf16[16,1024]{1,0:T(8,128)(2,1)S(1)}, bf16[16,1024]{1,0:T(8,128)(2,1)S(1)}, u32[]{:S(2)}, u32[]{:S(2)}) collective-permute-start(bf16[16,1024]{1,0:T(8,128)(2,1)S(1)} %broadcast_select_fusion.3), channel_id=1, source_target_pairs={{0,4},{4,8},{8,12},{1,5},{5,9},{9,13},{2,6},{6,10},{10,14},{3,7},{... | collective-permute-start | bytes 98312 | tf_op jit(solution)/shard_map/while/body/eval_jaxpr/ppermute | solution.py:12
  22.3 2.0 gather_fusion
  24.4 3.3 collective-permute-done.1
  28.8 2.3 collective-permute-done.2
  32.2 2.2 collective-permute-done.3
  34.7 10.0 %convolution_bitcast_fusion.2 = f32[3,16,1024]{2,1,0:T(8,128)S(1)} fusion(bf16[3,4096,1024]{2,1,0:T(8,128)(2,1)} %get-tuple-element.619, f32[4096]{0:T(1024)} %bitcast.78, f32[16]{0:T(128)S(1)} %add_rsqrt_fusion.3, bf16[16,8192]{1,0:T(8,128)(2,1)S(1)} %constant_dynamic-update-slice_fusion.23, s32[]{:T(128)S(6)} %select_n.272), kind=kOutput, calls=%fused_computation.11.clone.1 | convolution fusion | flops 402915328 | bytes 25510404 | tf_op jit(solution)/shard_map/while/body/eval_jaxpr/bd,jdc->jbc/dot_general | solution.py:88
  45.4 5.3 %fusion.45 = f32[16,4096]{1,0:T(8,128)} fusion(bf16[1024,4096]{1,0:T(8,128)(2,1)} %get-tuple-element.624, f32[16,1024]{1,0:T(8,128)S(1)} %get-tuple-element.535, f32[3,16,1024]{2,1,0:T(8,128)S(1)} %convolution_bitcast_fusion.2), kind=kOutput, calls=%fused_computation.29.clone.1 | convolution fusion | flops 134250496 | bytes 8781824 | tf_op jit(solution)/shard_map/while/body/eval_jaxpr/dot_general | solution.py:105
  54.6 16.6 %reduce-scatter.6.cloned.1.call-done = f32[16,1024]{1,0:T(8,128)} async-done(((f32[16,4096]{1,0:T(8,128)}), f32[16,1024]{1,0:T(8,128)}) %reduce-scatter.6.cloned.1.call-update) | async-done | bytes 65552 | tf_op jit(solution)/shard_map/while/body/eval_jaxpr/reduce_scatter | solution.py:106
  72.1 3.4 collective-permute-start
  78.3 2.0 gather_fusion
  80.4 3.3 collective-permute-done.1
  84.8 2.3 collective-permute-done.2
  88.2 2.2 collective-permute-done.3
  90.7 10.0 %convolution_bitcast_fusion.2 = f32[3,16,1024]{2,1,0:T(8,128)S(1)} fusion(bf16[3,4096,1024]{2,1,0:T(8,128)(2,1)} %get-tuple-element.619, f32[4096]{0:T(1024)} %bitcast.78, f32[16]{0:T(128)S(1)} %add_rsqrt_fusion.3, bf16[16,8192]{1,0:T(8,128)(2,1)S(1)} %constant_dynamic-update-slice_fusion.23, s32[]{:T(128)S(6)} %select_n.272), kind=kOutput, calls=%fused_computation.11.clone.1 | convolution fusion | flops 402915328 | bytes 25510404 | tf_op jit(solution)/shard_map/while/body/eval_jaxpr/bd,jdc->jbc/dot_general | solution.py:88
  101.4 5.3 %fusion.45 = f32[16,4096]{1,0:T(8,128)} fusion(bf16[1024,4096]{1,0:T(8,128)(2,1)} %get-tuple-element.624, f32[16,1024]{1,0:T(8,128)S(1)} %get-tuple-element.535, f32[3,16,1024]{2,1,0:T(8,128)S(1)} %convolution_bitcast_fusion.2), kind=kOutput, calls=%fused_computation.29.clone.1 | convolution fusion | flops 134250496 | bytes 8781824 | tf_op jit(solution)/shard_map/while/body/eval_jaxpr/dot_general | solution.py:105
  106.8 1.9 select_dynamic-update-slice_fusion.4
  110.6 15.5 %reduce-scatter.6.cloned.1.call-done = f32[16,1024]{1,0:T(8,128)} async-done(((f32[16,4096]{1,0:T(8,128)}), f32[16,1024]{1,0:T(8,128)}) %reduce-scatter.6.cloned.1.call-update) | async-done | bytes 65552 | tf_op jit(solution)/shard_map/while/body/eval_jaxpr/reduce_scatter | solution.py:106
  127.0 3.4 collective-permute-start
  133.2 2.0 gather_fusion
  135.3 3.3 collective-permute-done.1
  139.7 2.3 collective-permute-done.2
  143.0 2.2 collective-permute-done.3
  145.5 10.0 %convolution_bitcast_fusion.2 = f32[3,16,1024]{2,1,0:T(8,128)S(1)} fusion(bf16[3,4096,1024]{2,1,0:T(8,128)(2,1)} %get-tuple-element.619, f32[4096]{0:T(1024)} %bitcast.78, f32[16]{0:T(128)S(1)} %add_rsqrt_fusion.3, bf16[16,8192]{1,0:T(8,128)(2,1)S(1)} %constant_dynamic-update-slice_fusion.23, s32[]{:T(128)S(6)} %select_n.272), kind=kOutput, calls=%fused_computation.11.clone.1 | convolution fusion | flops 402915328 | bytes 25510404 | tf_op jit(solution)/shard_map/while/body/eval_jaxpr/bd,jdc->jbc/dot_general | solution.py:88
  156.3 5.3 %fusion.45 = f32[16,4096]{1,0:T(8,128)} fusion(bf16[1024,4096]{1,0:T(8,128)(2,1)} %get-tuple-element.624, f32[16,1024]{1,0:T(8,128)S(1)} %get-tuple-element.535, f32[3,16,1024]{2,1,0:T(8,128)S(1)} %convolution_bitcast_fusion.2), kind=kOutput, calls=%fused_computation.29.clone.1 | convolution fusion | flops 134250496 | bytes 8781824 | tf_op jit(solution)/shard_map/while/body/eval_jaxpr/dot_general | solution.py:105
  165.4 15.5 %reduce-scatter.6.cloned.1.call-done = f32[16,1024]{1,0:T(8,128)} async-done(((f32[16,4096]{1,0:T(8,128)}), f32[16,1024]{1,0:T(8,128)}) %reduce-scatter.6.cloned.1.call-update) | async-done | bytes 65552 | tf_op jit(solution)/shard_map/while/body/eval_jaxpr/reduce_scatter | solution.py:106
  181.8 3.4 collective-permute-start
  188.0 2.0 gather_fusion
  190.1 3.3 collective-permute-done.1
  194.5 2.3 collective-permute-done.2
  197.9 2.2 collective-permute-done.3
  200.4 10.0 %convolution_bitcast_fusion.2 = f32[3,16,1024]{2,1,0:T(8,128)S(1)} fusion(bf16[3,4096,1024]{2,1,0:T(8,128)(2,1)} %get-tuple-element.619, f32[4096]{0:T(1024)} %bitcast.78, f32[16]{0:T(128)S(1)} %add_rsqrt_fusion.3, bf16[16,8192]{1,0:T(8,128)(2,1)S(1)} %constant_dynamic-update-slice_fusion.23, s32[]{:T(128)S(6)} %select_n.272), kind=kOutput, calls=%fused_computation.11.clone.1 | convolution fusion | flops 402915328 | bytes 25510404 | tf_op jit(solution)/shard_map/while/body/eval_jaxpr/bd,jdc->jbc/dot_general | solution.py:88
  211.1 5.3 %fusion.45 = f32[16,4096]{1,0:T(8,128)} fusion(bf16[1024,4096]{1,0:T(8,128)(2,1)} %get-tuple-element.624, f32[16,1024]{1,0:T(8,128)S(1)} %get-tuple-element.535, f32[3,16,1024]{2,1,0:T(8,128)S(1)} %convolution_bitcast_fusion.2), kind=kOutput, calls=%fused_computation.29.clone.1 | convolution fusion | flops 134250496 | bytes 8781824 | tf_op jit(solution)/shard_map/while/body/eval_jaxpr/dot_general | solution.py:105
  220.3 15.5 %reduce-scatter.6.cloned.1.call-done = f32[16,1024]{1,0:T(8,128)} async-done(((f32[16,4096]{1,0:T(8,128)}), f32[16,1024]{1,0:T(8,128)}) %reduce-scatter.6.cloned.1.call-update) | async-done | bytes 65552 | tf_op jit(solution)/shard_map/while/body/eval_jaxpr/reduce_scatter | solution.py:106
  236.7 3.4 collective-permute-start
  242.9 2.0 gather_fusion
  245.0 3.3 collective-permute-done.1
  249.4 2.3 collective-permute-done.2
  252.7 2.2 collective-permute-done.3
  255.3 10.0 %convolution_bitcast_fusion.2 = f32[3,16,1024]{2,1,0:T(8,128)S(1)} fusion(bf16[3,4096,1024]{2,1,0:T(8,128)(2,1)} %get-tuple-element.619, f32[4096]{0:T(1024)} %bitcast.78, f32[16]{0:T(128)S(1)} %add_rsqrt_fusion.3, bf16[16,8192]{1,0:T(8,128)(2,1)S(1)} %constant_dynamic-update-slice_fusion.23, s32[]{:T(128)S(6)} %select_n.272), kind=kOutput, calls=%fused_computation.11.clone.1 | convolution fusion | flops 402915328 | bytes 25510404 | tf_op jit(solution)/shard_map/while/body/eval_jaxpr/bd,jdc->jbc/dot_general | solution.py:88
  266.0 5.3 %fusion.45 = f32[16,4096]{1,0:T(8,128)} fusion(bf16[1024,4096]{1,0:T(8,128)(2,1)} %get-tuple-element.624, f32[16,1024]{1,0:T(8,128)S(1)} %get-tuple-element.535, f32[3,16,1024]{2,1,0:T(8,128)S(1)} %convolution_bitcast_fusion.2), kind=kOutput, calls=%fused_computation.29.clone.1 | convolution fusion | flops 134250496 | bytes 8781824 | tf_op jit(solution)/shard_map/while/body/eval_jaxpr/dot_general | solution.py:105
  275.2 15.5 %reduce-scatter.6.cloned.1.call-done = f32[16,1024]{1,0:T(8,128)} async-done(((f32[16,4096]{1,0:T(8,128)}), f32[16,1024]{1,0:T(8,128)}) %reduce-scatter.6.cloned.1.call-update) | async-done | bytes 65552 | tf_op jit(solution)/shard_map/while/body/eval_jaxpr/reduce_scatter | solution.py:106
  291.6 3.4 collective-permute-start
  297.8 2.0 gather_fusion
  299.8 3.3 collective-permute-done.1
  304.2 2.3 collective-permute-done.2
  307.6 2.2 collective-permute-done.3
  310.1 10.0 %convolution_bitcast_fusion.2 = f32[3,16,1024]{2,1,0:T(8,128)S(1)} fusion(bf16[3,4096,1024]{2,1,0:T(8,128)(2,1)} %get-tuple-element.619, f32[4096]{0:T(1024)} %bitcast.78, f32[16]{0:T(128)S(1)} %add_rsqrt_fusion.3, bf16[16,8192]{1,0:T(8,128)(2,1)S(1)} %constant_dynamic-update-slice_fusion.23, s32[]{:T(128)S(6)} %select_n.272), kind=kOutput, calls=%fused_computation.11.clone.1 | convolution fusion | flops 402915328 | bytes 25510404 | tf_op jit(solution)/shard_map/while/body/eval_jaxpr/bd,jdc->jbc/dot_general | solution.py:88
  320.9 5.3 %fusion.45 = f32[16,4096]{1,0:T(8,128)} fusion(bf16[1024,4096]{1,0:T(8,128)(2,1)} %get-tuple-element.624, f32[16,1024]{1,0:T(8,128)S(1)} %get-tuple-element.535, f32[3,16,1024]{2,1,0:T(8,128)S(1)} %convolution_bitcast_fusion.2), kind=kOutput, calls=%fused_computation.29.clone.1 | convolution fusion | flops 134250496 | bytes 8781824 | tf_op jit(solution)/shard_map/while/body/eval_jaxpr/dot_general | solution.py:105
  330.0 15.5 %reduce-scatter.6.cloned.1.call-done = f32[16,1024]{1,0:T(8,128)} async-done(((f32[16,4096]{1,0:T(8,128)}), f32[16,1024]{1,0:T(8,128)}) %reduce-scatter.6.cloned.1.call-update) | async-done | bytes 65552 | tf_op jit(solution)/shard_map/while/body/eval_jaxpr/reduce_scatter | solution.py:106
  346.4 3.4 collective-permute-start
  352.6 2.0 gather_fusion
  354.7 3.3 collective-permute-done.1
  359.1 2.3 collective-permute-done.2
  362.5 2.2 collective-permute-done.3
  365.0 10.0 %convolution_bitcast_fusion.2 = f32[3,16,1024]{2,1,0:T(8,128)S(1)} fusion(bf16[3,4096,1024]{2,1,0:T(8,128)(2,1)} %get-tuple-element.619, f32[4096]{0:T(1024)} %bitcast.78, f32[16]{0:T(128)S(1)} %add_rsqrt_fusion.3, bf16[16,8192]{1,0:T(8,128)(2,1)S(1)} %constant_dynamic-update-slice_fusion.23, s32[]{:T(128)S(6)} %select_n.272), kind=kOutput, calls=%fused_computation.11.clone.1 | convolution fusion | flops 402915328 | bytes 25510404 | tf_op jit(solution)/shard_map/while/body/eval_jaxpr/bd,jdc->jbc/dot_general | solution.py:88
  375.7 5.3 %fusion.45 = f32[16,4096]{1,0:T(8,128)} fusion(bf16[1024,4096]{1,0:T(8,128)(2,1)} %get-tuple-element.624, f32[16,1024]{1,0:T(8,128)S(1)} %get-tuple-element.535, f32[3,16,1024]{2,1,0:T(8,128)S(1)} %convolution_bitcast_fusion.2), kind=kOutput, calls=%fused_computation.29.clone.1 | convolution fusion | flops 134250496 | bytes 8781824 | tf_op jit(solution)/shard_map/while/body/eval_jaxpr/dot_general | solution.py:105
  384.9 15.5 %reduce-scatter.6.cloned.1.call-done = f32[16,1024]{1,0:T(8,128)} async-done(((f32[16,4096]{1,0:T(8,128)}), f32[16,1024]{1,0:T(8,128)}) %reduce-scatter.6.cloned.1.call-update) | async-done | bytes 65552 | tf_op jit(solution)/shard_map/while/body/eval_jaxpr/reduce_scatter | solution.py:106
  401.2 6.6 %all_gather.3 = bf16[2,32,4096]{2,1,0:T(8,128)(2,1)S(1)} all-gather(bf16[2,32,1024]{2,1,0:T(8,128)(2,1)S(1)} %get-tuple-element.311), channel_id=1, replica_groups=mesh['groups'=2,'segment'=4,'inner'=4] {'inner'}, dimensions={2}, use_global_device_ids=true | all-gather | bytes 655360 | tf_op jit(solution)/shard_map/all_gather | solution.py:126
  409.0 2.6 copy.27
  411.6 6.7 %all-reduce.1 = (f32[2,32]{1,0:T(2,128)S(1)}, f32[2,32]{1,0:T(2,128)S(1)}) all-reduce(f32[2,32]{1,0:T(2,128)S(1)} %get-tuple-element.375, f32[2,32]{1,0:T(2,128)S(1)} %get-tuple-element.374), channel_id=1, replica_groups=mesh['groups'=2,'segment'=4,'inner'=4] {'inner'}, use_global_device_ids=true, to_apply=%region_11.12 | all-reduce | flops 128 | bytes 1024 | tf_op jit(solution)/shard_map/psum | solution.py:136
  418.3 11.7 %all-reduce = f32[2,32]{1,0:T(2,128)S(1)} all-reduce(f32[2,32]{1,0:T(2,128)S(1)} %subtract_select_fusion), channel_id=4, replica_groups=mesh['groups'=2,'segment'=4,'inner'=4] {'segment'}, use_global_device_ids=true, to_apply=%region_14.15.clone | all-reduce | flops 64 | bytes 512
  (286 shorter events, 77.2 us)
Async XLA Ops:
  8.0 400.0 %copy-start = (bf16[4096,128]{1,0:T(8,128)(2,1)S(1)}, bf16[4096,128]{1,0:T(8,128)(2,1)}, u32[]{:S(2)}) copy-start(bf16[4096,128]{1,0:T(8,128)(2,1)} %param.27) | copy-start | bytes 3145732
  14.5 393.5 %copy-start.3 = (f32[4096]{0:T(1024)S(1)}, f32[4096]{0:T(1024)}, u32[]{:S(2)}) copy-start(f32[4096]{0:T(1024)} %param.26) | copy-start | bytes 49156
  14.5 415.6 %copy-start.4 = (u32[32]{0:T(128)S(1)}, u32[32]{0:T(128)}, u32[]{:S(2)}) copy-start(u32[32]{0:T(128)} %constant.216) | copy-start | bytes 388
  14.5 56.7 %reduce-scatter.6.cloned.1.call-start = ((), (), s32[]{:S(2)}) async-start(), calls=%async_computation.3 | async-start | bytes 327680 | tf_op jit(solution)/shard_map/while/body/eval_jaxpr/reduce_scatter | solution.py:106
  14.6 9.7 %collective-permute-start = (bf16[16,1024]{1,0:T(8,128)(2,1)S(1)}, bf16[16,1024]{1,0:T(8,128)(2,1)S(1)}, u32[]{:S(2)}, u32[]{:S(2)}) collective-permute-start(bf16[16,1024]{1,0:T(8,128)(2,1)S(1)} %broadcast_select_fusion.3), channel_id=1, source_target_pairs={{0,4},{4,8},{8,12},{1,5},{5,9},{9,13},{2,6},{6,10},{10,14},{3,7},{... | collective-permute-start | bytes 98312 | tf_op jit(solution)/shard_map/while/body/eval_jaxpr/ppermute | solution.py:12
  24.4 3.3 collective-permute-start.1
  27.7 3.3 collective-permute-start.2
  31.1 3.3 collective-permute-start.3
  34.4 10.2 %copy-start.1 = (f32[1,8,1024]{2,1,0:T(8,128)S(1)}, f32[1,8,1024]{2,1,0:T(8,128)}, u32[]{:S(2)}) copy-start(f32[1,8,1024]{2,1,0:T(8,128)} %get-tuple-element.621) | copy-start | bytes 98308 | tf_op jit(solution)/shard_map/while
  34.4 10.2 %copy-start.2 = (f32[8,1024]{1,0:T(8,128)S(1)}, f32[8,1024]{1,0:T(8,128)}, u32[]{:S(2)}) copy-start(f32[8,1024]{1,0:T(8,128)} %get-tuple-element.622) | copy-start | bytes 98308 | tf_op jit(solution)/shard_map/while
  72.1 54.0 %reduce-scatter.6.cloned.1.call-start = ((), (), s32[]{:S(2)}) async-start(), calls=%async_computation.3 | async-start | bytes 327680 | tf_op jit(solution)/shard_map/while/body/eval_jaxpr/reduce_scatter | solution.py:106
  72.1 8.2 %collective-permute-start = (bf16[16,1024]{1,0:T(8,128)(2,1)S(1)}, bf16[16,1024]{1,0:T(8,128)(2,1)S(1)}, u32[]{:S(2)}, u32[]{:S(2)}) collective-permute-start(bf16[16,1024]{1,0:T(8,128)(2,1)S(1)} %broadcast_select_fusion.3), channel_id=1, source_target_pairs={{0,4},{4,8},{8,12},{1,5},{5,9},{9,13},{2,6},{6,10},{10,14},{3,7},{... | collective-permute-start | bytes 98312 | tf_op jit(solution)/shard_map/while/body/eval_jaxpr/ppermute | solution.py:12
  80.4 3.3 collective-permute-start.1
  83.7 3.3 collective-permute-start.2
  87.1 3.3 collective-permute-start.3
  90.4 10.2 %copy-start.1 = (f32[1,8,1024]{2,1,0:T(8,128)S(1)}, f32[1,8,1024]{2,1,0:T(8,128)}, u32[]{:S(2)}) copy-start(f32[1,8,1024]{2,1,0:T(8,128)} %get-tuple-element.621) | copy-start | bytes 98308 | tf_op jit(solution)/shard_map/while
  90.4 10.2 %copy-start.2 = (f32[8,1024]{1,0:T(8,128)S(1)}, f32[8,1024]{1,0:T(8,128)}, u32[]{:S(2)}) copy-start(f32[8,1024]{1,0:T(8,128)} %get-tuple-element.622) | copy-start | bytes 98308 | tf_op jit(solution)/shard_map/while
  126.9 54.0 %reduce-scatter.6.cloned.1.call-start = ((), (), s32[]{:S(2)}) async-start(), calls=%async_computation.3 | async-start | bytes 327680 | tf_op jit(solution)/shard_map/while/body/eval_jaxpr/reduce_scatter | solution.py:106
  127.0 8.2 %collective-permute-start = (bf16[16,1024]{1,0:T(8,128)(2,1)S(1)}, bf16[16,1024]{1,0:T(8,128)(2,1)S(1)}, u32[]{:S(2)}, u32[]{:S(2)}) collective-permute-start(bf16[16,1024]{1,0:T(8,128)(2,1)S(1)} %broadcast_select_fusion.3), channel_id=1, source_target_pairs={{0,4},{4,8},{8,12},{1,5},{5,9},{9,13},{2,6},{6,10},{10,14},{3,7},{... | collective-permute-start | bytes 98312 | tf_op jit(solution)/shard_map/while/body/eval_jaxpr/ppermute | solution.py:12
  135.3 3.3 collective-permute-start.1
  138.6 3.3 collective-permute-start.2
  141.9 3.3 collective-permute-start.3
  145.3 10.2 %copy-start.1 = (f32[1,8,1024]{2,1,0:T(8,128)S(1)}, f32[1,8,1024]{2,1,0:T(8,128)}, u32[]{:S(2)}) copy-start(f32[1,8,1024]{2,1,0:T(8,128)} %get-tuple-element.621) | copy-start | bytes 98308 | tf_op jit(solution)/shard_map/while
  145.3 10.2 %copy-start.2 = (f32[8,1024]{1,0:T(8,128)S(1)}, f32[8,1024]{1,0:T(8,128)}, u32[]{:S(2)}) copy-start(f32[8,1024]{1,0:T(8,128)} %get-tuple-element.622) | copy-start | bytes 98308 | tf_op jit(solution)/shard_map/while
  181.8 54.0 %reduce-scatter.6.cloned.1.call-start = ((), (), s32[]{:S(2)}) async-start(), calls=%async_computation.3 | async-start | bytes 327680 | tf_op jit(solution)/shard_map/while/body/eval_jaxpr/reduce_scatter | solution.py:106
  181.8 8.2 %collective-permute-start = (bf16[16,1024]{1,0:T(8,128)(2,1)S(1)}, bf16[16,1024]{1,0:T(8,128)(2,1)S(1)}, u32[]{:S(2)}, u32[]{:S(2)}) collective-permute-start(bf16[16,1024]{1,0:T(8,128)(2,1)S(1)} %broadcast_select_fusion.3), channel_id=1, source_target_pairs={{0,4},{4,8},{8,12},{1,5},{5,9},{9,13},{2,6},{6,10},{10,14},{3,7},{... | collective-permute-start | bytes 98312 | tf_op jit(solution)/shard_map/while/body/eval_jaxpr/ppermute | solution.py:12
  190.1 3.3 collective-permute-start.1
  193.5 3.3 collective-permute-start.2
  196.8 3.3 collective-permute-start.3
  200.1 10.2 %copy-start.1 = (f32[1,8,1024]{2,1,0:T(8,128)S(1)}, f32[1,8,1024]{2,1,0:T(8,128)}, u32[]{:S(2)}) copy-start(f32[1,8,1024]{2,1,0:T(8,128)} %get-tuple-element.621) | copy-start | bytes 98308 | tf_op jit(solution)/shard_map/while
  200.1 10.2 %copy-start.2 = (f32[8,1024]{1,0:T(8,128)S(1)}, f32[8,1024]{1,0:T(8,128)}, u32[]{:S(2)}) copy-start(f32[8,1024]{1,0:T(8,128)} %get-tuple-element.622) | copy-start | bytes 98308 | tf_op jit(solution)/shard_map/while
  236.6 54.0 %reduce-scatter.6.cloned.1.call-start = ((), (), s32[]{:S(2)}) async-start(), calls=%async_computation.3 | async-start | bytes 327680 | tf_op jit(solution)/shard_map/while/body/eval_jaxpr/reduce_scatter | solution.py:106
  236.7 8.2 %collective-permute-start = (bf16[16,1024]{1,0:T(8,128)(2,1)S(1)}, bf16[16,1024]{1,0:T(8,128)(2,1)S(1)}, u32[]{:S(2)}, u32[]{:S(2)}) collective-permute-start(bf16[16,1024]{1,0:T(8,128)(2,1)S(1)} %broadcast_select_fusion.3), channel_id=1, source_target_pairs={{0,4},{4,8},{8,12},{1,5},{5,9},{9,13},{2,6},{6,10},{10,14},{3,7},{... | collective-permute-start | bytes 98312 | tf_op jit(solution)/shard_map/while/body/eval_jaxpr/ppermute | solution.py:12
  245.0 3.3 collective-permute-start.1
  248.3 3.3 collective-permute-start.2
  251.6 3.3 collective-permute-start.3
  255.0 10.2 %copy-start.1 = (f32[1,8,1024]{2,1,0:T(8,128)S(1)}, f32[1,8,1024]{2,1,0:T(8,128)}, u32[]{:S(2)}) copy-start(f32[1,8,1024]{2,1,0:T(8,128)} %get-tuple-element.621) | copy-start | bytes 98308 | tf_op jit(solution)/shard_map/while
  255.0 10.2 %copy-start.2 = (f32[8,1024]{1,0:T(8,128)S(1)}, f32[8,1024]{1,0:T(8,128)}, u32[]{:S(2)}) copy-start(f32[8,1024]{1,0:T(8,128)} %get-tuple-element.622) | copy-start | bytes 98308 | tf_op jit(solution)/shard_map/while
  291.5 54.0 %reduce-scatter.6.cloned.1.call-start = ((), (), s32[]{:S(2)}) async-start(), calls=%async_computation.3 | async-start | bytes 327680 | tf_op jit(solution)/shard_map/while/body/eval_jaxpr/reduce_scatter | solution.py:106
  291.6 8.2 %collective-permute-start = (bf16[16,1024]{1,0:T(8,128)(2,1)S(1)}, bf16[16,1024]{1,0:T(8,128)(2,1)S(1)}, u32[]{:S(2)}, u32[]{:S(2)}) collective-permute-start(bf16[16,1024]{1,0:T(8,128)(2,1)S(1)} %broadcast_select_fusion.3), channel_id=1, source_target_pairs={{0,4},{4,8},{8,12},{1,5},{5,9},{9,13},{2,6},{6,10},{10,14},{3,7},{... | collective-permute-start | bytes 98312 | tf_op jit(solution)/shard_map/while/body/eval_jaxpr/ppermute | solution.py:12
  299.8 3.3 collective-permute-start.1
  303.2 3.3 collective-permute-start.2
  306.5 3.3 collective-permute-start.3
  309.8 10.2 %copy-start.1 = (f32[1,8,1024]{2,1,0:T(8,128)S(1)}, f32[1,8,1024]{2,1,0:T(8,128)}, u32[]{:S(2)}) copy-start(f32[1,8,1024]{2,1,0:T(8,128)} %get-tuple-element.621) | copy-start | bytes 98308 | tf_op jit(solution)/shard_map/while
  309.8 10.2 %copy-start.2 = (f32[8,1024]{1,0:T(8,128)S(1)}, f32[8,1024]{1,0:T(8,128)}, u32[]{:S(2)}) copy-start(f32[8,1024]{1,0:T(8,128)} %get-tuple-element.622) | copy-start | bytes 98308 | tf_op jit(solution)/shard_map/while
  346.3 54.0 %reduce-scatter.6.cloned.1.call-start = ((), (), s32[]{:S(2)}) async-start(), calls=%async_computation.3 | async-start | bytes 327680 | tf_op jit(solution)/shard_map/while/body/eval_jaxpr/reduce_scatter | solution.py:106
  346.4 8.2 %collective-permute-start = (bf16[16,1024]{1,0:T(8,128)(2,1)S(1)}, bf16[16,1024]{1,0:T(8,128)(2,1)S(1)}, u32[]{:S(2)}, u32[]{:S(2)}) collective-permute-start(bf16[16,1024]{1,0:T(8,128)(2,1)S(1)} %broadcast_select_fusion.3), channel_id=1, source_target_pairs={{0,4},{4,8},{8,12},{1,5},{5,9},{9,13},{2,6},{6,10},{10,14},{3,7},{... | collective-permute-start | bytes 98312 | tf_op jit(solution)/shard_map/while/body/eval_jaxpr/ppermute | solution.py:12
  354.7 3.3 collective-permute-start.1
  358.0 3.3 collective-permute-start.2
  361.4 3.3 collective-permute-start.3
  364.7 10.2 %copy-start.1 = (f32[1,8,1024]{2,1,0:T(8,128)S(1)}, f32[1,8,1024]{2,1,0:T(8,128)}, u32[]{:S(2)}) copy-start(f32[1,8,1024]{2,1,0:T(8,128)} %get-tuple-element.621) | copy-start | bytes 98308 | tf_op jit(solution)/shard_map/while
  364.7 10.2 %copy-start.2 = (f32[8,1024]{1,0:T(8,128)S(1)}, f32[8,1024]{1,0:T(8,128)}, u32[]{:S(2)}) copy-start(f32[8,1024]{1,0:T(8,128)} %get-tuple-element.622) | copy-start | bytes 98308 | tf_op jit(solution)/shard_map/while
  401.2 30.7 %reduce-scatter.4.cloned.1.call-start = ((), (), s32[]{:S(2)}) async-start(), calls=%async_computation.2 | async-start | bytes 40960 | tf_op jit(solution)/shard_map/reduce_scatter | solution.py:141
Sparse Core Ops, SparseCore 0:
  50.9 20.2 reduce-scatter.5
  106.9 19.1 reduce-scatter.5
  161.7 19.1 reduce-scatter.5
  216.6 19.1 reduce-scatter.5
  271.4 19.1 reduce-scatter.5
  326.3 19.1 reduce-scatter.5
  381.1 19.1 reduce-scatter.5
Sparse Core Ops, SparseCore 1:
  409.1 19.8 reduce-scatter.3
